TPU v7x, 32 devices: a whole 2x2x4 slice. The times are simulated.
32 devices in a mesh: dp: 4 (over y, x), tensor: 8 (over z, core).
Axes of the slice: x: 2, y: 2, z: 4, core: 2. Of those that a mesh axis runs over, the one named last changes fastest.
Arguments:
- tokens: bfloat16 [2048, 2048], P(('dp', 'tensor')), may hold values from -6 to 6
- cotangent: bfloat16 [2048, 2048], P(('dp', 'tensor')), may hold values from -6 to 6
- w_query: bfloat16 [2048, 2048], P(None, 'tensor'), may hold values from -0.125 to 0.125
- w_key: bfloat16 [2048, 2048], P(None, 'tensor'), may hold values from -0.125 to 0.125
- w_value: bfloat16 [2048, 2048], P(None, 'tensor'), may hold values from -0.125 to 0.125
- w_out: bfloat16 [2048, 2048], P('tensor'), may hold values from -0.125 to 0.125
- w_gate: bfloat16 [2048, 8192], P(None, 'tensor'), may hold values from -0.125 to 0.125
- w_up: bfloat16 [2048, 8192], P(None, 'tensor'), may hold values from -0.125 to 0.125
- w_down: bfloat16 [8192, 2048], P('tensor'), may hold values from -0.0625 to 0.0625
- q_gain: float32 [2048], P('tensor'), may hold values from 0.1 to 1.9
- k_gain: float32 [2048], P('tensor'), may hold values from 0.1 to 1.9
- attn_gain: float32 [2048], replicated, may hold values from 0.1 to 1.9
- ffn_gain: float32 [2048], replicated, may hold values from 0.1 to 1.9
Outputs:
- layer_out: float32 [2048, 2048], P(('dp', 'tensor'))
- grad_tokens: float32 [2048, 2048], P(('dp', 'tensor'))
- grad_w_query: float32 [2048, 2048], P(None, 'tensor')
- grad_w_key: float32 [2048, 2048], P(None, 'tensor')
- grad_w_value: float32 [2048, 2048], P(None, 'tensor')
- grad_w_out: float32 [2048, 2048], P('tensor')
- grad_w_gate: float32 [2048, 8192], P(None, 'tensor')
- grad_w_up: float32 [2048, 8192], P(None, 'tensor')
- grad_w_down: float32 [8192, 2048], P('tensor')
- grad_q_gain: float32 [2048], P('tensor')
- grad_k_gain: float32 [2048], P('tensor')
- grad_attn_gain: float32 [2048], replicated
- grad_ffn_gain: float32 [2048], replicated
All inputs are finite; a program needn't handle non-finite values.
Results may differ from a plain program's by a relative error of at most 0.015.
Values may be sent and summed in bfloat16 or wider, within the bound.
No kernel may reach another device: no remote copies, remote signals or barrier semaphores. Data moves between devices by JAX's collectives and lax.ppermute only.
A program may use at most 192 MiB of HBM per device.

v0:
```python
import math
import jax
import jax.numpy as jnp
from jax import lax
from jax.sharding import PartitionSpec as P

HD = 128
SEQ = 256
epsilon = 1e-06
rope_base = 500000.0


def rope_tables(length, head_width):
    half_width = head_width // 2
    exponent = jnp.arange(half_width, dtype=jnp.float32) * (2.0 / head_width)
    frequency = rope_base ** (-exponent)
    angles = jnp.arange(length, dtype=jnp.float32)[:, None] * frequency[None, :]
    cos_table = jnp.concatenate([jnp.cos(angles), jnp.cos(angles)], axis=1)
    sin_table = jnp.concatenate([jnp.sin(angles), jnp.sin(angles)], axis=1)
    return (cos_table[None, :, None, :], sin_table[None, :, None, :])


def rotate(field, cos_table, sin_table):
    half_width = field.shape[-1] // 2
    turned = jnp.concatenate([-field[..., half_width:], field[..., :half_width]], axis=-1)
    return field * cos_table + turned * sin_table


def unrotate(grad_field, cos_table, sin_table):
    half_width = grad_field.shape[-1] // 2
    moved = grad_field * sin_table
    back_part = jnp.concatenate([moved[..., half_width:], -moved[..., :half_width]], axis=-1)
    return grad_field * cos_table + back_part


def row_scale(matrix):
    return lax.rsqrt(jnp.mean(matrix * matrix, axis=1, keepdims=True) + epsilon)


def norm_back(grad_normed, normed, inverse):
    return inverse * (grad_normed - normed * jnp.mean(grad_normed * normed, axis=1, keepdims=True))


def product(left, right):
    return jnp.dot(left, right, preferred_element_type=jnp.float32)


def times_transposed(left, right):
    return lax.dot_general(
        left, right, (((1,), (1,)), ((), ())), preferred_element_type=jnp.float32
    )


def transposed_times(left, right):
    return lax.dot_general(
        left, right, (((0,), (0,)), ((), ())), preferred_element_type=jnp.float32
    )


def shards(
    tokens,
    cotangent,
    w_query,
    w_key,
    w_value,
    w_out,
    w_gate,
    w_up,
    w_down,
    q_gain,
    k_gain,
    attn_gain,
    ffn_gain,
):
    row_count = tokens.shape[0]
    model_width = tokens.shape[1]
    row_start = lax.axis_index("tensor") * row_count
    gathered = lax.all_gather(tokens, "tensor", axis=0, tiled=True)
    group_rows = gathered.shape[0]
    seq_count = group_rows // SEQ
    local_width = w_query.shape[1]
    local_heads = local_width // HD
    head_shape = (seq_count, SEQ, local_heads, HD)
    cos_table, sin_table = rope_tables(SEQ, HD)
    score_scale = 1.0 / math.sqrt(HD)
    query = product(gathered, w_query)
    keys = product(gathered, w_key)
    values = product(gathered, w_value).astype(jnp.bfloat16)
    q_squares, k_squares = lax.psum(
        (jnp.sum(query * query, axis=1), jnp.sum(keys * keys, axis=1)), "tensor"
    )
    q_inverse = lax.rsqrt(q_squares[:, None] / model_width + epsilon)
    k_inverse = lax.rsqrt(k_squares[:, None] / model_width + epsilon)
    q_normed = query * q_inverse
    k_normed = keys * k_inverse
    q_rot = rotate((q_normed * q_gain).reshape(head_shape), cos_table, sin_table).astype(
        jnp.bfloat16
    )
    k_rot = rotate((k_normed * k_gain).reshape(head_shape), cos_table, sin_table).astype(
        jnp.bfloat16
    )
    v_heads = values.reshape(head_shape)
    causal = jnp.arange(SEQ)[:, None] >= jnp.arange(SEQ)[None, :]
    scores = (
        jnp.einsum("sqhd,skhd->shqk", q_rot, k_rot, preferred_element_type=jnp.float32)
        * score_scale
    )
    scores = jnp.where(causal, scores, -1e30)
    top_score = jnp.max(scores, axis=3, keepdims=True)
    shifted = jnp.exp(scores - top_score)
    total = jnp.sum(shifted, axis=3, keepdims=True)
    probs = (shifted / total).astype(jnp.bfloat16)
    log_total = top_score + jnp.log(total)
    attended = jnp.einsum("shqk,skhd->sqhd", probs, v_heads, preferred_element_type=jnp.float32)
    attended = attended.astype(jnp.bfloat16).reshape(group_rows, local_width)
    attn_full = lax.psum(product(attended, w_out), "tensor")
    inverse_full = row_scale(attn_full)
    normed_full = attn_full * inverse_full
    mixed_full = gathered.astype(jnp.float32) + normed_full * attn_gain
    mixed_b = mixed_full.astype(jnp.bfloat16)
    a_inverse = lax.dynamic_slice_in_dim(inverse_full, row_start, row_count, 0)
    a_normed = lax.dynamic_slice_in_dim(normed_full, row_start, row_count, 0)
    mixed = lax.dynamic_slice_in_dim(mixed_full, row_start, row_count, 0)
    gate = product(mixed_b, w_gate)
    up_proj = product(mixed_b, w_up)
    sigmoid_gate = jax.nn.sigmoid(gate)
    activated = gate * sigmoid_gate
    swiglu = (activated * up_proj).astype(jnp.bfloat16)
    ffn_rows = lax.psum_scatter(product(swiglu, w_down), "tensor", scatter_dimension=0, tiled=True)
    m_inverse = row_scale(ffn_rows)
    m_normed = ffn_rows * m_inverse
    layer_out = mixed + m_normed * ffn_gain
    grad_out = cotangent.astype(jnp.float32)
    ffn_gain_part = jnp.sum(grad_out * m_normed, axis=0)
    grad_ffn = norm_back(grad_out * ffn_gain, m_normed, m_inverse).astype(jnp.bfloat16)
    grad_ffn_all = lax.all_gather(grad_ffn, "tensor", axis=0, tiled=True)
    grad_w_down = transposed_times(swiglu, grad_ffn_all)
    grad_swiglu = times_transposed(grad_ffn_all, w_down)
    grad_gate = (grad_swiglu * up_proj * sigmoid_gate * (1.0 + gate * (1.0 - sigmoid_gate))).astype(
        jnp.bfloat16
    )
    grad_up = (grad_swiglu * activated).astype(jnp.bfloat16)
    grad_w_gate = transposed_times(mixed_b, grad_gate)
    grad_w_up = transposed_times(mixed_b, grad_up)
    grad_mixed = grad_out + lax.psum_scatter(
        times_transposed(grad_gate, w_gate) + times_transposed(grad_up, w_up),
        "tensor",
        scatter_dimension=0,
        tiled=True,
    )
    attn_gain_part = jnp.sum(grad_mixed * a_normed, axis=0)
    grad_attn = norm_back(grad_mixed * attn_gain, a_normed, a_inverse).astype(jnp.bfloat16)
    grad_attn_all = lax.all_gather(grad_attn, "tensor", axis=0, tiled=True)
    grad_w_out = transposed_times(attended, grad_attn_all)
    grad_attended = times_transposed(grad_attn_all, w_out).astype(jnp.bfloat16)
    grad_heads = grad_attended.reshape(head_shape)
    prob_back = jnp.where(causal, jnp.exp(scores - log_total), 0.0)
    grad_values = jnp.einsum(
        "shqk,sqhd->skhd", probs, grad_heads, preferred_element_type=jnp.float32
    ).astype(jnp.bfloat16)
    grad_probs = jnp.einsum(
        "sqhd,skhd->shqk", grad_heads, v_heads, preferred_element_type=jnp.float32
    )
    inner = jnp.sum(prob_back * grad_probs, axis=3, keepdims=True)
    grad_scores = (prob_back * (grad_probs - inner) * score_scale).astype(jnp.bfloat16)
    grad_qrot = jnp.einsum(
        "shqk,skhd->sqhd", grad_scores, k_rot, preferred_element_type=jnp.float32
    )
    grad_krot = jnp.einsum(
        "shqk,sqhd->skhd", grad_scores, q_rot, preferred_element_type=jnp.float32
    )
    grad_qn = unrotate(grad_qrot, cos_table, sin_table).reshape(group_rows, local_width)
    grad_kn = unrotate(grad_krot, cos_table, sin_table).reshape(group_rows, local_width)
    grad_q_gain = jnp.sum(grad_qn * q_normed, axis=0)
    grad_k_gain = jnp.sum(grad_kn * k_normed, axis=0)
    q_target = grad_qn * q_gain
    k_target = grad_kn * k_gain
    q_inner, k_inner, grad_attn_gain, grad_ffn_gain = lax.psum(
        (
            jnp.sum(q_target * q_normed, axis=1),
            jnp.sum(k_target * k_normed, axis=1),
            attn_gain_part,
            ffn_gain_part,
        ),
        "tensor",
    )
    grad_query = (q_inverse * (q_target - q_normed * (q_inner[:, None] / model_width))).astype(
        jnp.bfloat16
    )
    grad_keys = (k_inverse * (k_target - k_normed * (k_inner[:, None] / model_width))).astype(
        jnp.bfloat16
    )
    grad_values = grad_values.reshape(group_rows, local_width)
    grad_w_query = transposed_times(gathered, grad_query)
    grad_w_key = transposed_times(gathered, grad_keys)
    grad_w_value = transposed_times(gathered, grad_values)
    grad_tokens = grad_mixed + lax.psum_scatter(
        times_transposed(grad_query, w_query)
        + times_transposed(grad_keys, w_key)
        + times_transposed(grad_values, w_value),
        "tensor",
        scatter_dimension=0,
        tiled=True,
    )
    (
        grad_w_query,
        grad_w_key,
        grad_w_value,
        grad_w_out,
        grad_w_gate,
        grad_w_up,
        grad_w_down,
        grad_q_gain,
        grad_k_gain,
        grad_attn_gain,
        grad_ffn_gain,
    ) = lax.psum(
        (
            grad_w_query,
            grad_w_key,
            grad_w_value,
            grad_w_out,
            grad_w_gate,
            grad_w_up,
            grad_w_down,
            grad_q_gain,
            grad_k_gain,
            grad_attn_gain,
            grad_ffn_gain,
        ),
        "dp",
    )
    return (
        layer_out,
        grad_tokens,
        grad_w_query,
        grad_w_key,
        grad_w_value,
        grad_w_out,
        grad_w_gate,
        grad_w_up,
        grad_w_down,
        grad_q_gain,
        grad_k_gain,
        grad_attn_gain,
        grad_ffn_gain,
    )


def solution(mesh):
    placed = (
        P(("dp", "tensor"), None),
        P(("dp", "tensor"), None),
        P(None, "tensor"),
        P(None, "tensor"),
        P(None, "tensor"),
        P("tensor", None),
        P(None, "tensor"),
        P(None, "tensor"),
        P("tensor", None),
        P("tensor"),
        P("tensor"),
        P(),
        P(),
    )
    return jax.shard_map(
        shards,
        mesh=mesh,
        in_specs=placed,
        out_specs=(
            P(("dp", "tensor"), None),
            P(("dp", "tensor"), None),
            P(None, "tensor"),
            P(None, "tensor"),
            P(None, "tensor"),
            P("tensor", None),
            P(None, "tensor"),
            P(None, "tensor"),
            P("tensor", None),
            P("tensor"),
            P("tensor"),
            P(),
            P(),
        ),
        check_vma=False,
    )
```

profile of v0, /device:TPU:0, one launch (start us, length us, event | category | flops | bytes accessed | tf_op | source)
XLA Modules:
  0.0 1108.2 jit_solution(12256830166530808767)
XLA Ops:
  9.6 31.9 %all-gather.4.cloned.1.call-done = bf16[512,2048]{1,0:T(8,128)(2,1)} async-done(((bf16[64,2048]{1,0:T(8,128)(2,1)}), bf16[512,2048]{1,0:T(8,128)(2,1)}) %all-gather.4.cloned.1.call-update) | async-done | bytes 2097168 | tf_op jit(solution)/shard_map/all_gather | solution.py:78
  41.5 3.4 convolution_convert_fusion.3
  44.9 1.0 reshape.124
  46.0 2.9 multiply_reduce_fusion.9
  48.8 1.6 multiply_reduce_fusion.10
  50.4 15.8 %all-reduce.1 = (f32[512]{0:T(512)S(1)}, f32[512]{0:T(512)}) all-reduce(f32[512]{0:T(512)S(1)} %get-tuple-element.87, f32[512]{0:T(512)S(1)} %get-tuple-element.89), channel_id=1, replica_groups=mesh['dp'=4,'tensor'=8] {'tensor'}, use_global_device_ids=true, to_apply=%region_1.0 | all-reduce | flops 1024 | bytes 8192 | tf_op jit(solution)/shard_map/psum | solution.py:89
  67.5 2.0 multiply_multiply_fusion
  69.4 2.2 reshape.126
  71.6 1.1 copy.50
  74.5 2.2 reshape.125
  76.7 1.2 copy.47
  82.1 1.1 copy.57
  83.3 4.0 fusion.42
  87.9 94.3 %all-reduce.7.cloned.1.call-done = f32[512,2048]{1,0:T(8,128)} async-done(((f32[512,2048]{1,0:T(8,128)}), f32[512,2048]{1,0:T(8,128)}) %all-reduce.7.cloned.1.call-update) | async-done | bytes 4194320 | tf_op jit(solution)/shard_map/psum | solution.py:116
  182.1 2.7 multiply_reduce_fusion
  185.6 4.7 fusion.60
  190.3 2.4 fusion.66
  193.3 3.7 multiply_convert_fusion.2
  198.0 4.4 fusion.67
  202.5 50.1 %reduce-scatter.4.cloned.1.call-done = f32[64,2048]{1,0:T(8,128)} async-done(((f32[512,2048]{1,0:T(8,128)}), f32[64,2048]{1,0:T(8,128)}) %reduce-scatter.4.cloned.1.call-update) | async-done | bytes 524304 | tf_op jit(solution)/shard_map/reduce_scatter | solution.py:129
  252.5 1.2 multiply_reduce_fusion.8
  253.7 1.8 fusion.19
  255.6 2.3 fusion.18
  258.1 27.6 %all-gather.6.cloned.1.call-done = bf16[512,2048]{1,0:T(8,128)(2,1)} async-done(((bf16[64,2048]{1,0:T(8,128)(2,1)}), bf16[512,2048]{1,0:T(8,128)(2,1)}) %all-gather.6.cloned.1.call-update) | async-done | bytes 2097168 | tf_op jit(solution)/shard_map/all_gather | solution.py:136
  285.7 7.1 multiply_convert_fusion
  292.8 2.4 fusion.68
  295.7 4.4 convolution_add_fusion
  300.2 1.3 dynamic-slice.3
  301.5 48.2 %reduce-scatter.6.cloned.1.call-done = f32[64,2048]{1,0:T(8,128)} async-done(((f32[512,2048]{1,0:T(8,128)}), f32[64,2048]{1,0:T(8,128)}) %reduce-scatter.6.cloned.1.call-update) | async-done | bytes 524304 | tf_op jit(solution)/shard_map/reduce_scatter | solution.py:145
  349.6 1.9 multiply_reduce_fusion.2
  351.6 2.1 multiply_convert_fusion.5
  353.7 27.7 %all-gather.8.cloned.1.call-done = bf16[512,2048]{1,0:T(8,128)(2,1)} async-done(((bf16[64,2048]{1,0:T(8,128)(2,1)}), bf16[512,2048]{1,0:T(8,128)(2,1)}) %all-gather.8.cloned.1.call-update) | async-done | bytes 2097168 | tf_op jit(solution)/shard_map/all_gather | solution.py:153
  381.4 3.3 convolution_convert_fusion.1
  384.7 1.7 reshape.128
  386.5 1.8 copy.64
  388.3 2.1 fusion.8
  390.4 2.3 fusion.49
  392.7 1.8 copy.66
  394.5 3.8 convolution_bitcast_fusion.4
  398.3 4.4 broadcast_multiply_fusion.1
  402.6 1.2 fusion.61
  403.8 1.1 fusion.62
  407.6 27.8 %all-reduce = (f32[512]{0:T(512)S(1)}, f32[512]{0:T(512)S(1)}, f32[2048]{0:T(1024)S(1)}, f32[2048]{0:T(1024)S(1)}) all-reduce(f32[512]{0:T(512)S(1)} %get-tuple-element.44, f32[512]{0:T(512)S(1)} %get-tuple-element.42, f32[2048]{0:T(1024)S(1)} %copy-done.44, f32[2048]{0:T(1024)S(1)} %copy-done.43), channel_id=1, replica_groups=mesh['dp'=4,'tensor'=8] {'tensor'}, use_global_device_ids=true, to_apply=%region_15.16 | all-reduce | flops 5120 | bytes 40960 | tf_op jit(solution)/shard_map/psum | solution.py:178
  435.4 1.3 multiply_convert_fusion.4
  436.8 1.4 multiply_convert_fusion.3
  440.8 2.8 add_add_fusion
  443.7 7.8 fusion.72
  451.6 5.8 fusion.71
  457.4 5.8 fusion.73
  463.2 2.1 fusion.40
  465.2 2.0 convolution_bitcast_fusion.1
  467.3 2.0 convolution_bitcast_fusion.2
  469.3 2.1 convolution_bitcast_fusion
  471.4 16.9 %all-reduce.2 = (f32[256]{0:T(256)}, f32[256]{0:T(256)}, f32[2048]{0:T(1024)}, f32[2048]{0:T(1024)}) all-reduce(f32[256]{0:T(256)S(1)} %get-tuple-element.43, f32[256]{0:T(256)S(1)} %get-tuple-element.41, f32[2048]{0:T(1024)S(1)} %get-tuple-element.49, f32[2048]{0:T(1024)S(1)} %get-tuple-element.50), channel_id=1, replica_groups=mesh['dp'=4,'tensor'=8] {'dp'}, use_global_device_ids=true, to_apply=%region_27.28 | all-reduce | flops 4608 | bytes 36864 | tf_op jit(solution)/shard_map/psum | solution.py:217
  488.3 3.6 reduce-scatter.8.cloned.1.call-done
  491.9 1.9 fusion.53
  493.8 580.4 %all-reduce.9.cloned.1.call-done = (f32[2048,256]{0,1:T(8,128)}, f32[2048,256]{0,1:T(8,128)}, f32[2048,256]{0,1:T(8,128)}, f32[256,2048]{1,0:T(8,128)}, f32[2048...) async-done(((f32[2048,256]{0,1:T(8,128)}, f32[2048,256]{0,1:T(8,128)}, f32[2048,256]{0,1:T(8,128)}, f32[256,2048]{1,0:T(8,128)}, f32[2048,1024]{1,0:T(8,128)}, ...) | async-done | bytes 33554448 | tf_op jit(solution)/shard_map/psum | solution.py:217
  1074.2 3.0 copy.67
  1077.2 1.8 copy.68
  1079.0 3.0 copy.69
  1082.1 1.3 copy.110
  1083.4 9.1 copy.111
  1092.6 4.3 copy.112
  1097.8 3.4 copy.113
  (179 shorter events, 19.7 us)
Async XLA Ops:
  7.2 41.7 %copy-start = (bf16[2048,256]{1,0:T(8,128)(2,1)S(1)}, bf16[2048,256]{1,0:T(8,128)(2,1)}, u32[]{:S(2)}) copy-start(bf16[2048,256]{1,0:T(8,128)(2,1)} %param.15) | copy-start | bytes 3145732
  7.2 34.3 %all-gather.4.cloned.1.call-start = ((), (), s32[]{:S(2)}) async-start(), calls=%async_computation.3 | async-start | bytes 2359296 | tf_op jit(solution)/shard_map/all_gather | solution.py:78
  7.9 174.2 %all-reduce.7.cloned.1.call-start = ((), (), s32[]{:S(2)}) async-start(), calls=%async_computation.4 | async-start | bytes 8388608 | tf_op jit(solution)/shard_map/psum | solution.py:116
  41.5 4.4 copy-start.2
  46.0 34.4 %copy-start.22 = (bf16[2,256,2,128]{3,2,1,0:T(2,128)(2,1)}, bf16[2,256,2,128]{3,2,1,0:T(2,128)(2,1)S(1)}, u32[]{:S(2)}) copy-start(bf16[2,256,2,128]{3,2,1,0:T(2,128)(2,1)S(1)} %reshape.124) | copy-start | bytes 786436
  48.8 18.6 %copy-start.47 = (f32[256]{0:T(256)S(1)}, f32[256]{0:T(256)}, u32[]{:S(2)}) copy-start(f32[256]{0:T(256)} %param.23) | copy-start | bytes 3076
  66.9 6.6 copy-start.41
  67.5 6.1 copy-start.45
  71.6 2.0 copy-start.8
  76.6 1.3 copy-start.13
  76.6 1.4 copy-start.14
  76.7 1.4 copy-start.30
  76.7 1.5 copy-start.31
  76.7 1.5 copy-start.36
  78.4 1.9 copy-start.28
  78.4 1.9 copy-start.29
  83.2 4.1 copy-start.15
  87.3 97.5 %copy-start.38 = (f32[2048]{0:T(1024)S(1)}, f32[2048]{0:T(1024)}, u32[]{:S(2)}) copy-start(f32[2048]{0:T(1024)} %param.24) | copy-start | bytes 24580
  87.3 165.2 %reduce-scatter.4.cloned.1.call-start = ((), (), s32[]{:S(2)}) async-start(), calls=%async_computation.5 | async-start | bytes 4718592 | tf_op jit(solution)/shard_map/reduce_scatter | solution.py:129
  182.1 3.4 copy-start.3
  185.6 4.7 copy-start.49
  185.6 4.8 copy-start.51
  190.3 2.4 copy-start.26
  190.3 2.9 copy-start.53
  193.3 3.7 copy-start.61
  193.3 4.7 copy-start.50
  202.4 51.3 %copy-start.5 = (bf16[64,2048]{1,0:T(8,128)(2,1)S(1)}, bf16[64,2048]{1,0:T(8,128)(2,1)}, u32[]{:S(2)}) copy-start(bf16[64,2048]{1,0:T(8,128)(2,1)} %param.14) | copy-start | bytes 786436
  202.4 83.2 %all-gather.6.cloned.1.call-start = ((), (), s32[]{:S(2)}) async-start(), calls=%async_computation.6 | async-start | bytes 2359296 | tf_op jit(solution)/shard_map/all_gather | solution.py:136
  257.9 91.8 %reduce-scatter.6.cloned.1.call-start = ((), (), s32[]{:S(2)}) async-start(), calls=%async_computation.7 | async-start | bytes 4718592 | tf_op jit(solution)/shard_map/reduce_scatter | solution.py:145
  285.7 7.1 copy-start.52
  292.8 2.4 copy-start.56
  292.8 2.4 copy-start.58
  292.8 2.9 copy-start.54
  300.2 81.3 %all-gather.8.cloned.1.call-start = ((), (), s32[]{:S(2)}) async-start(), calls=%async_computation.8 | async-start | bytes 2359296 | tf_op jit(solution)/shard_map/all_gather | solution.py:153
  353.7 138.2 %reduce-scatter.8.cloned.1.call-start = ((), (), s32[]{:S(2)}) async-start(), calls=%async_computation.9 | async-start | bytes 4718592 | tf_op jit(solution)/shard_map/reduce_scatter | solution.py:197
  402.6 2.2 copy-start.34
  402.6 2.3 copy-start.35
  404.9 1.0 copy-start.7
  404.9 1.0 copy-start.40
  405.5 1.3 copy-start.9
  405.5 1.3 copy-start.42
  405.5 1.3 copy-start.46
  405.9 1.7 copy-start.43
  405.9 1.7 copy-start.44
  436.7 2.2 copy-start.17
  438.2 1.3 copy-start.32
  439.5 1.3 copy-start.33
  443.7 630.5 %all-reduce.9.cloned.1.call-start = ((), (), s32[]{:S(2)}) async-start(), calls=%async_computation.10 | async-start | bytes 67108864 | tf_op jit(solution)/shard_map/psum | solution.py:217
  443.7 7.8 copy-start.27
  443.7 7.8 copy-start.57
  451.5 5.8 copy-start.55
  451.5 5.8 copy-start.60
  457.4 5.8 copy-start.16
  457.4 5.8 copy-start.23
  463.2 2.1 copy-start.20
  465.2 2.0 copy-start.18
  471.4 20.5 %copy-start.6 = (f32[64,2048]{1,0:T(8,128)S(1)}, f32[64,2048]{1,0:T(8,128)}, u32[]{:S(2)}) copy-start(f32[64,2048]{1,0:T(8,128)} %reduce-scatter.6.cloned.1.call-done) | copy-start | bytes 1572868
  1074.2 3.0 copy-start.25
  1079.0 3.0 copy-start.24
  1082.1 10.5 slice-start.2
  1083.4 9.1 slice-start.3
  1083.4 13.4 %slice-start = ((s8[8388608]{0:T(1024)(128)(4,1)}), s8[4194304]{0:T(1024)(128)(4,1)S(1)}, s32[]{:S(2)}) async-start(s8[8388608]{0:T(1024)(128)(4,1)} %bitcast.88), calls=%async_computation.11 | async-start | bytes 8388608
  1092.6 5.2 slice-start.1
  1097.8 3.4 copy-start.1
  (10 other events, 8.6 us)
Sparse Core Ops, SparseCore 0:
  9.6 31.8 all-gather.3
  87.5 94.6 all-reduce.6
  202.5 49.9 reduce-scatter.3
  258.0 27.6 all-gather.5
  300.3 49.3 reduce-scatter.5
  353.8 27.6 all-gather.7
  443.8 48.0 reduce-scatter.7
  497.8 576.3 all-reduce.8
where the time goes:
time: 1110 us
  waiting for transfers between devices  864 us (78%)
  matrix products  85.4 us (8%)
  blocking collectives  60.5 us (5%)
  local copies, waits for them, and re-layouts  51.2 us (5%)
  other arithmetic  30.8 us (3%)
  between operations  15 us (1%)
    psum x1, waiting for transfers between devices, shards(): lax.psum((grad_w_query, grad_w_key, grad_w_value, grad_w_out, grad_w_gate...  580 us
    psum x1, waiting for transfers between devices, shards(): attn_full = lax.psum(product(attended, w_out), 'tensor')  94.3 us
    reduce_scatter x1, waiting for transfers between devices, shards(): lax.psum_scatter(product(swiglu, w_down), 'tensor', scatter_dimension=0,...  50.1 us
    reduce_scatter x1, waiting for transfers between devices, shards(): lax.psum_scatter(times_transposed(grad_gate, w_gate) + times_transposed(g...  48.2 us
    unnamed x141, local copies, waits for them, and re-layouts  35 us
    all_gather x1, waiting for transfers between devices, shards(): gathered = lax.all_gather(tokens, 'tensor', axis=0, tiled=True)  31.9 us
    psum x1, blocking collectives, shards(): lax.psum((jnp.sum(q_target * q_normed, axis=1), jnp.sum(k_target * k_norm...  27.8 us
    all_gather x1, waiting for transfers between devices, shards(): grad_attn_all = lax.all_gather(grad_attn, 'tensor', axis=0, tiled=True)  27.7 us
  transfers between devices with their start and end apart: 8, of which 8 were waited for; matrix products, arithmetic and copies ran while one was open for 3% of the time, Pallas kernels for 0%

commit v1 on v0

--- a/solution.py
+++ b/solution.py
@@ -113,7 +113,7 @@
     log_total = top_score + jnp.log(total)
     attended = jnp.einsum("shqk,skhd->sqhd", probs, v_heads, preferred_element_type=jnp.float32)
     attended = attended.astype(jnp.bfloat16).reshape(group_rows, local_width)
-    attn_full = lax.psum(product(attended, w_out), "tensor")
+    attn_full = jnp.sum(lax.all_gather(product(attended, w_out), "tensor"), axis=0)
     inverse_full = row_scale(attn_full)
     normed_full = attn_full * inverse_full
     mixed_full = gathered.astype(jnp.float32) + normed_full * attn_gain

time: 1110 us -> 1320 us (1.19)
  waiting for transfers between devices: 864 us -> 1050 us
  other arithmetic: 30.8 us -> 44.9 us
    all_gather x0 -> x1, waiting for transfers between devices: none -> 286 us  [shards(): lax.all_gather(product(attended, w_out), 'tensor')]
    psum x1 -> x0, waiting for transfers between devices: 94.3 us -> none  [shards(): attn_full = lax.psum(product(attended, w_out), 'tensor')]
    reduce_sum x0 -> x1, other arithmetic: none -> 14.1 us  [shards(): jnp.sum(lax.all_gather(product(attended, w_out), 'tensor'), axis=0)]
  transfers between devices with their start and end apart: 8 -> 8, of which waited for: 8 -> 8; matrix products, arithmetic and copies ran while one was open for 3% -> 2% of each run, Pallas kernels for 0% -> 0%
where the time goes in v1:
time: 1320 us; the launch traced here: 1310 us
  waiting for transfers between devices  1050 us (80%)
  matrix products  85.4 us (6%)
  blocking collectives  60.5 us (5%)
  local copies, waits for them, and re-layouts  51.2 us (4%)
  other arithmetic  44.9 us (3%)
  between operations  15 us (1%)
    psum x1, waiting for transfers between devices, shards(): lax.psum((grad_w_query, grad_w_key, grad_w_value, grad_w_out, grad_w_gate...  580 us
    all_gather x1, waiting for transfers between devices, shards(): lax.all_gather(product(attended, w_out), 'tensor')  286 us
    reduce_scatter x1, waiting for transfers between devices, shards(): lax.psum_scatter(product(swiglu, w_down), 'tensor', scatter_dimension=0,...  48.2 us
    reduce_scatter x1, waiting for transfers between devices, shards(): lax.psum_scatter(times_transposed(grad_gate, w_gate) + times_transposed(g...  48.2 us
    unnamed x141, local copies, waits for them, and re-layouts  35 us
    all_gather x1, waiting for transfers between devices, shards(): gathered = lax.all_gather(tokens, 'tensor', axis=0, tiled=True)  31.9 us
    psum x1, blocking collectives, shards(): lax.psum((jnp.sum(q_target * q_normed, axis=1), jnp.sum(k_target * k_norm...  27.8 us
    all_gather x1, waiting for transfers between devices, shards(): grad_attn_all = lax.all_gather(grad_attn, 'tensor', axis=0, tiled=True)  27.7 us
  transfers between devices with their start and end apart: 8, of which 8 were waited for; matrix products, arithmetic and copies ran while one was open for 2% of the time, Pallas kernels for 0%

profile of v1, /device:TPU:0, one launch (start us, length us, event | category | flops | bytes accessed | tf_op | source)
XLA Modules:
  0.0 1312.7 jit_solution(12331498837870572952)
XLA Ops:
  9.6 31.9 %all-gather.6.cloned.1.call-done = bf16[512,2048]{1,0:T(8,128)(2,1)} async-done(((bf16[64,2048]{1,0:T(8,128)(2,1)}), bf16[512,2048]{1,0:T(8,128)(2,1)}) %all-gather.6.cloned.1.call-update) | async-done | bytes 2097168 | tf_op jit(solution)/shard_map/all_gather | solution.py:78
  41.5 3.4 convolution_convert_fusion.3
  46.0 2.9 multiply_reduce_fusion.9
  48.8 1.6 multiply_reduce_fusion.10
  50.4 15.8 %all-reduce.1 = (f32[512]{0:T(512)S(1)}, f32[512]{0:T(512)}) all-reduce(f32[512]{0:T(512)S(1)} %get-tuple-element.87, f32[512]{0:T(512)S(1)} %get-tuple-element.89), channel_id=1, replica_groups=mesh['dp'=4,'tensor'=8] {'tensor'}, use_global_device_ids=true, to_apply=%region_1.0 | all-reduce | flops 1024 | bytes 8192 | tf_op jit(solution)/shard_map/psum | solution.py:89
  67.5 2.0 multiply_multiply_fusion
  69.4 2.2 reshape.126
  71.6 1.1 copy.50
  74.5 2.2 reshape.125
  76.7 1.2 copy.47
  82.1 1.1 copy.57
  83.3 4.0 fusion.42
  87.9 286.4 %all-gather.12.cloned.1.call-done = f32[4096,2048]{1,0:T(8,128)} async-done(((f32[512,2048]{1,0:T(8,128)}), f32[4096,2048]{1,0:T(8,128)}) %all-gather.12.cloned.1.call-update) | async-done | bytes 33554448 | tf_op jit(solution)/shard_map/all_gather | solution.py:116
  374.2 14.1 %reduce_sum.138 = f32[512,2048]{1,0:T(8,128)} reduce(f32[8,512,2048]{2,1,0:T(8,128)} %bitcast.89, f32[]{:T(128)} %constant.13.clone.1), dimensions={0}, to_apply=%region_6.7 | reduce | flops 7340032 | bytes 37748740 | tf_op jit(solution)/shard_map/reduce_sum | solution.py:116
  388.4 2.7 multiply_reduce_fusion
  391.8 4.7 fusion.60
  396.6 2.4 fusion.66
  399.5 3.7 multiply_convert_fusion.2
  404.3 4.4 fusion.67
  408.7 48.2 %reduce-scatter.4.cloned.1.call-done = f32[64,2048]{1,0:T(8,128)} async-done(((f32[512,2048]{1,0:T(8,128)}), f32[64,2048]{1,0:T(8,128)}) %reduce-scatter.4.cloned.1.call-update) | async-done | bytes 524304 | tf_op jit(solution)/shard_map/reduce_scatter | solution.py:129
  456.9 1.2 multiply_reduce_fusion.8
  458.1 1.8 fusion.19
  460.0 2.3 fusion.18
  462.5 27.6 %all-gather.8.cloned.1.call-done = bf16[512,2048]{1,0:T(8,128)(2,1)} async-done(((bf16[64,2048]{1,0:T(8,128)(2,1)}), bf16[512,2048]{1,0:T(8,128)(2,1)}) %all-gather.8.cloned.1.call-update) | async-done | bytes 2097168 | tf_op jit(solution)/shard_map/all_gather | solution.py:136
  490.1 7.1 multiply_convert_fusion
  497.2 2.4 fusion.68
  500.2 4.4 convolution_add_fusion
  504.6 1.3 dynamic-slice.3
  505.9 48.2 %reduce-scatter.6.cloned.1.call-done = f32[64,2048]{1,0:T(8,128)} async-done(((f32[512,2048]{1,0:T(8,128)}), f32[64,2048]{1,0:T(8,128)}) %reduce-scatter.6.cloned.1.call-update) | async-done | bytes 524304 | tf_op jit(solution)/shard_map/reduce_scatter | solution.py:145
  554.0 1.9 multiply_reduce_fusion.2
  556.0 2.1 multiply_convert_fusion.5
  558.1 27.7 %all-gather.10.cloned.1.call-done = bf16[512,2048]{1,0:T(8,128)(2,1)} async-done(((bf16[64,2048]{1,0:T(8,128)(2,1)}), bf16[512,2048]{1,0:T(8,128)(2,1)}) %all-gather.10.cloned.1.call-update) | async-done | bytes 2097168 | tf_op jit(solution)/shard_map/all_gather | solution.py:153
  585.8 3.3 convolution_convert_fusion.1
  589.1 1.7 reshape.128
  590.9 1.8 copy.64
  592.7 2.1 fusion.8
  594.8 2.3 fusion.49
  597.1 1.8 copy.66
  598.9 3.8 convolution_bitcast_fusion.4
  602.7 4.4 broadcast_multiply_fusion.1
  607.0 1.2 fusion.61
  608.2 1.1 fusion.62
  612.0 27.8 %all-reduce = (f32[512]{0:T(512)S(1)}, f32[512]{0:T(512)S(1)}, f32[2048]{0:T(1024)S(1)}, f32[2048]{0:T(1024)S(1)}) all-reduce(f32[512]{0:T(512)S(1)} %get-tuple-element.44, f32[512]{0:T(512)S(1)} %get-tuple-element.42, f32[2048]{0:T(1024)S(1)} %copy-done.44, f32[2048]{0:T(1024)S(1)} %copy-done.43), channel_id=1, replica_groups=mesh['dp'=4,'tensor'=8] {'tensor'}, use_global_device_ids=true, to_apply=%region_15.16 | all-reduce | flops 5120 | bytes 40960 | tf_op jit(solution)/shard_map/psum | solution.py:178
  639.8 1.3 multiply_convert_fusion.4
  641.2 1.4 multiply_convert_fusion.3
  645.3 2.8 add_add_fusion
  648.2 7.8 fusion.72
  656.0 5.8 fusion.71
  661.8 5.8 fusion.73
  667.6 2.1 fusion.40
  669.7 2.0 convolution_bitcast_fusion.1
  671.7 2.0 convolution_bitcast_fusion.2
  673.7 2.1 convolution_bitcast_fusion
  675.8 16.9 %all-reduce.2 = (f32[256]{0:T(256)}, f32[256]{0:T(256)}, f32[2048]{0:T(1024)}, f32[2048]{0:T(1024)}) all-reduce(f32[256]{0:T(256)S(1)} %get-tuple-element.43, f32[256]{0:T(256)S(1)} %get-tuple-element.41, f32[2048]{0:T(1024)S(1)} %get-tuple-element.49, f32[2048]{0:T(1024)S(1)} %get-tuple-element.50), channel_id=1, replica_groups=mesh['dp'=4,'tensor'=8] {'dp'}, use_global_device_ids=true, to_apply=%region_27.28 | all-reduce | flops 4608 | bytes 36864 | tf_op jit(solution)/shard_map/psum | solution.py:217
  692.7 3.6 reduce-scatter.8.cloned.1.call-done
  696.3 1.9 fusion.53
  698.2 580.4 %all-reduce.6.cloned.1.call-done = (f32[2048,256]{0,1:T(8,128)}, f32[2048,256]{0,1:T(8,128)}, f32[2048,256]{0,1:T(8,128)}, f32[256,2048]{1,0:T(8,128)}, f32[2048...) async-done(((f32[2048,256]{0,1:T(8,128)}, f32[2048,256]{0,1:T(8,128)}, f32[2048,256]{0,1:T(8,128)}, f32[256,2048]{1,0:T(8,128)}, f32[2048,1024]{1,0:T(8,128)}, ...) | async-done | bytes 33554448 | tf_op jit(solution)/shard_map/psum | solution.py:217
  1278.6 3.0 copy.67
  1281.7 1.8 copy.68
  1283.5 3.0 copy.69
  1286.5 1.3 copy.109
  1287.8 9.1 copy.110
  1297.0 4.3 copy.111
  1302.2 3.4 copy.112
  (180 shorter events, 20.7 us)
Async XLA Ops:
  7.2 41.7 %copy-start = (bf16[2048,256]{1,0:T(8,128)(2,1)S(1)}, bf16[2048,256]{1,0:T(8,128)(2,1)}, u32[]{:S(2)}) copy-start(bf16[2048,256]{1,0:T(8,128)(2,1)} %param.15) | copy-start | bytes 3145732
  7.2 34.3 %all-gather.6.cloned.1.call-start = ((), (), s32[]{:S(2)}) async-start(), calls=%async_computation.3 | async-start | bytes 2359296 | tf_op jit(solution)/shard_map/all_gather | solution.py:78
  7.9 366.3 %all-gather.12.cloned.1.call-start = ((), (), s32[]{:S(2)}) async-start(), calls=%async_computation.9 | async-start | bytes 37748736 | tf_op jit(solution)/shard_map/all_gather | solution.py:116
  41.5 4.4 copy-start.3
  46.0 34.4 %copy-start.22 = (bf16[2,256,2,128]{3,2,1,0:T(2,128)(2,1)}, bf16[2,256,2,128]{3,2,1,0:T(2,128)(2,1)S(1)}, u32[]{:S(2)}) copy-start(bf16[2,256,2,128]{3,2,1,0:T(2,128)(2,1)S(1)} %reshape.124) | copy-start | bytes 786436
  48.8 18.6 %copy-start.47 = (f32[256]{0:T(256)S(1)}, f32[256]{0:T(256)}, u32[]{:S(2)}) copy-start(f32[256]{0:T(256)} %param.23) | copy-start | bytes 3076
  66.9 6.6 copy-start.41
  67.5 6.1 copy-start.45
  71.6 2.0 copy-start.8
  76.6 1.3 copy-start.13
  76.6 1.4 copy-start.14
  76.6 1.4 copy-start.30
  76.6 1.5 copy-start.31
  76.6 1.5 copy-start.36
  78.4 1.9 copy-start.28
  78.4 1.9 copy-start.29
  83.2 4.1 copy-start.15
  87.3 369.6 %reduce-scatter.4.cloned.1.call-start = ((), (), s32[]{:S(2)}) async-start(), calls=%async_computation.4 | async-start | bytes 4718592 | tf_op jit(solution)/shard_map/reduce_scatter | solution.py:129
  374.2 16.8 %copy-start.38 = (f32[2048]{0:T(1024)S(1)}, f32[2048]{0:T(1024)}, u32[]{:S(2)}) copy-start(f32[2048]{0:T(1024)} %param.24) | copy-start | bytes 24580
  388.4 3.4 copy-start.2
  391.8 4.7 copy-start.49
  391.8 4.8 copy-start.51
  396.6 2.4 copy-start.26
  396.6 2.9 copy-start.53
  399.5 3.7 copy-start.61
  399.5 4.7 copy-start.50
  408.6 49.5 %copy-start.5 = (bf16[64,2048]{1,0:T(8,128)(2,1)S(1)}, bf16[64,2048]{1,0:T(8,128)(2,1)}, u32[]{:S(2)}) copy-start(bf16[64,2048]{1,0:T(8,128)(2,1)} %param.14) | copy-start | bytes 786436
  408.7 81.4 %all-gather.8.cloned.1.call-start = ((), (), s32[]{:S(2)}) async-start(), calls=%async_computation.5 | async-start | bytes 2359296 | tf_op jit(solution)/shard_map/all_gather | solution.py:136
  462.3 91.8 %reduce-scatter.6.cloned.1.call-start = ((), (), s32[]{:S(2)}) async-start(), calls=%async_computation.6 | async-start | bytes 4718592 | tf_op jit(solution)/shard_map/reduce_scatter | solution.py:145
  490.1 7.1 copy-start.52
  497.2 2.4 copy-start.56
  497.2 2.4 copy-start.58
  497.2 2.9 copy-start.54
  504.6 81.3 %all-gather.10.cloned.1.call-start = ((), (), s32[]{:S(2)}) async-start(), calls=%async_computation.7 | async-start | bytes 2359296 | tf_op jit(solution)/shard_map/all_gather | solution.py:153
  558.1 138.3 %reduce-scatter.8.cloned.1.call-start = ((), (), s32[]{:S(2)}) async-start(), calls=%async_computation.8 | async-start | bytes 4718592 | tf_op jit(solution)/shard_map/reduce_scatter | solution.py:197
  607.0 2.2 copy-start.34
  607.0 2.3 copy-start.35
  609.3 1.0 copy-start.7
  609.3 1.0 copy-start.40
  609.9 1.3 copy-start.9
  609.9 1.3 copy-start.42
  609.9 1.3 copy-start.46
  610.4 1.7 copy-start.43
  610.4 1.7 copy-start.44
  641.2 2.2 copy-start.17
  642.6 1.3 copy-start.32
  644.0 1.3 copy-start.33
  648.1 630.5 %all-reduce.6.cloned.1.call-start = ((), (), s32[]{:S(2)}) async-start(), calls=%async_computation.10 | async-start | bytes 67108864 | tf_op jit(solution)/shard_map/psum | solution.py:217
  648.2 7.8 copy-start.27
  648.2 7.8 copy-start.57
  656.0 5.8 copy-start.55
  656.0 5.8 copy-start.60
  661.8 5.8 copy-start.16
  661.8 5.8 copy-start.23
  667.6 2.1 copy-start.20
  669.7 2.0 copy-start.18
  675.8 20.5 %copy-start.6 = (f32[64,2048]{1,0:T(8,128)S(1)}, f32[64,2048]{1,0:T(8,128)}, u32[]{:S(2)}) copy-start(f32[64,2048]{1,0:T(8,128)} %reduce-scatter.6.cloned.1.call-done) | copy-start | bytes 1572868
  1278.6 3.0 copy-start.25
  1283.5 3.0 copy-start.24
  1286.5 10.5 slice-start.2
  1287.8 9.1 slice-start.3
  1287.8 13.4 %slice-start = ((s8[8388608]{0:T(1024)(128)(4,1)}), s8[4194304]{0:T(1024)(128)(4,1)S(1)}, s32[]{:S(2)}) async-start(s8[8388608]{0:T(1024)(128)(4,1)} %bitcast.90), calls=%async_computation.11 | async-start | bytes 8388608
  1297.0 5.2 slice-start.1
  1302.2 3.4 copy-start.1
  (10 other events, 8.6 us)
Sparse Core Ops, SparseCore 0:
  9.6 31.8 all-gather.5
  87.5 286.7 all-gather.11
  408.8 48.0 reduce-scatter.3
  462.4 27.6 all-gather.7
  504.7 49.3 reduce-scatter.5
  558.2 27.6 all-gather.9
  648.2 48.0 reduce-scatter.7
  702.2 576.3 all-reduce.5
